TPU v7x, 32 devices: a whole 2x2x4 slice. The times are simulated.
32 devices in a mesh: clus: 8 (over y, x, core), lab: 4 (over z).
Axes of the slice: x: 2, y: 2, z: 4, core: 2. Of those that a mesh axis runs over, the one named last changes fastest.
Arguments:
- queries: bfloat16 [4096, 768], P(('clus', 'lab')), may hold values from -6 to 6
- visits: int32 [4096, 4], P(('clus', 'lab')), may hold values from 0 to 15, all different within a row; in each aligned block of 128 rows (0 to 127, 128 to 255, ...) at most 64 rows name the same one
- positives: int32 [4096, 4], P(('clus', 'lab')), may hold values from 0 to 4095
- weights: bfloat16 [16, 4096, 768], P('clus', 'lab'), may hold values from -0.21875 to 0.21875
- momentum: float32 [16, 4096, 768], P('clus', 'lab'), may hold values from -24 to 24
Outputs:
- query_grad: float32 [4096, 768], P(('clus', 'lab'))
- weights_new: bfloat16 [16, 4096, 768], P('clus', 'lab')
- momentum_new: float32 [16, 4096, 768], P('clus', 'lab')
Inputs may be any that keep to these rules, and one draw needn't show every extreme that they name: `visits`: each query names 4 different clusters; among the 128 queries of one device at most 64 visit any one cluster.
All inputs are finite; a program needn't handle non-finite values.
Results may differ from a plain program's by a relative error of at most 0.006.
Values may be sent and summed in bfloat16 or wider, within the bound.
A program may use at most 128 MiB of HBM per device.

v0:
```python
import jax
import jax.numpy as jnp
from jax import lax
from jax.sharding import PartitionSpec as P

momentum_decay = 0.9
step_rate = 0.002


def shards(queries, visits, positives, weights, momentum):
    n_clus = lax.axis_size("clus")
    q_count, width = queries.shape
    visit_count = visits.shape[1]
    clus_local, block_size, _ = weights.shape
    all_clusters = clus_local * n_clus
    capacity = 2 * q_count * visit_count // all_clusters
    flat_visits = visits.reshape(-1)
    one_hot = (flat_visits[:, None] == jnp.arange(all_clusters, dtype=jnp.int32)[None, :]).astype(
        jnp.int32
    )
    before = jnp.cumsum(one_hot, axis=0) - one_hot
    ranks = jnp.sum(before * one_hot, axis=1)
    slots = flat_visits * capacity + ranks
    repeated = jnp.repeat(queries, visit_count, axis=0)
    outbox = jnp.zeros((all_clusters * capacity, width), jnp.bfloat16).at[slots].set(repeated)
    outbox = outbox.reshape(all_clusters, capacity, width)
    out_tags = (
        jnp.full((all_clusters * capacity,), -1, jnp.int32).at[slots].set(positives.reshape(-1))
    )
    out_tags = out_tags.reshape(all_clusters, capacity)
    landed, landed_tags = (
        lax.all_to_all(outbox, "clus", split_axis=0, concat_axis=1, tiled=True),
        lax.all_to_all(out_tags, "clus", split_axis=0, concat_axis=1, tiled=True),
    )
    arrived, label_tag = (
        lax.all_gather(landed, "lab", axis=1, tiled=True),
        lax.all_gather(landed_tags, "lab", axis=1, tiled=True),
    )
    offsets = lax.axis_index("lab") * block_size + jnp.arange(block_size, dtype=jnp.int32)
    logits = jnp.einsum("crd,cbd->crb", arrived, weights, preferred_element_type=jnp.float32)
    target = (label_tag[:, :, None] == offsets[None, None, :]).astype(jnp.float32)
    live = label_tag >= 0
    grad = jnp.where(live[:, :, None], jax.nn.sigmoid(logits) - target, 0.0).astype(jnp.bfloat16)
    partial_grad = jnp.einsum("crb,cbd->crd", grad, weights, preferred_element_type=jnp.float32)
    label_grad = jnp.einsum("crb,crd->cbd", grad, arrived, preferred_element_type=jnp.float32)
    folded = lax.psum_scatter(
        partial_grad.astype(jnp.bfloat16), "lab", scatter_dimension=1, tiled=True
    ).astype(jnp.float32)
    homed = lax.all_to_all(
        folded.astype(jnp.bfloat16), "clus", split_axis=1, concat_axis=0, tiled=True
    ).astype(folded.dtype)
    homed = homed.reshape(all_clusters * capacity, width)
    query_grad = jnp.sum(homed[slots].reshape(q_count, visit_count, width), axis=1)
    momentum_new = momentum_decay * momentum + label_grad
    weights_new = (weights.astype(jnp.float32) - step_rate * momentum_new).astype(jnp.bfloat16)
    return (query_grad, weights_new, momentum_new)


def solution(mesh):
    in_specs = (
        P(("clus", "lab"), None),
        P(("clus", "lab"), None),
        P(("clus", "lab"), None),
        P("clus", "lab", None),
        P("clus", "lab", None),
    )
    out_specs = (P(("clus", "lab"), None), P("clus", "lab", None), P("clus", "lab", None))
    return jax.shard_map(shards, mesh=mesh, in_specs=in_specs, out_specs=out_specs, check_vma=False)
```

profile of v0, /device:TPU:25, one launch (start us, length us, event | category | flops | bytes accessed | tf_op | source)
XLA Modules:
  0.0 329.9 jit_solution(8040990217270346746)
XLA Ops:
  7.2 0.8 copy.28
  8.2 0.7 broadcast_multiply_fusion
  8.9 1.1 reduce-window.6
  10.1 0.2 slice_reduce_fusion
  10.3 0.1 copy.27
  10.6 1.1 broadcast_in_dim.31
  11.7 0.2 reshape.108
  12.0 3.0 scatter_custom_fusion.1
  15.0 23.9 %all_to_all.46 = bf16[16,64,768]{2,1,0:T(8,128)(2,1)S(1)} all-to-all(bf16[16,64,768]{2,1,0:T(8,128)(2,1)S(1)} %bitcast.40), channel_id=1, replica_groups=mesh['clus'=8,'lab'=4] {'clus'}, dimensions={0} | all-to-all | bytes 3145728 | tf_op jit(solution)/shard_map/all_to_all | solution.py:32
  38.9 1.3 copy.33
  40.2 0.1 copy.31
  40.4 2.4 scatter_custom_fusion
  42.9 0.7 reshape.117
  43.6 4.4 %all-to-all-start = ((s32[8,1,128]{2,1,0:T(1,128)}), s32[8,1,128]{2,1,0:T(1,128)S(1)}, u32[]{:S(2)}, u32[]{:S(2)}) async-start(s32[8,1,128]{2,1,0:T(1,128)} %reshape.117), calls=%async_computation | async-start | bytes 8192 | tf_op jit(solution)/shard_map/all_to_all | solution.py:33
  48.1 4.3 %all-to-all-done = s32[8,1,128]{2,1,0:T(1,128)S(1)} async-done(((s32[8,1,128]{2,1,0:T(1,128)}), s32[8,1,128]{2,1,0:T(1,128)S(1)}, u32[]{:S(2)}, u32[]{:S(2)}) %all-to-all-start) | async-done | bytes 4128 | tf_op jit(solution)/shard_map/all_to_all | solution.py:33
  52.4 0.5 broadcast.68
  52.9 0.7 reduce.2
  53.8 14.4 %all_gather.6 = s32[2,2048]{1,0:T(2,128)S(1)} all-gather(s32[2,512]{1,0:T(2,128)S(1)} %all_to_all.37), channel_id=1, replica_groups=mesh['clus'=8,'lab'=4] {'lab'}, dimensions={1}, use_global_device_ids=true | all-gather | bytes 20480 | tf_op jit(solution)/shard_map/all_gather | solution.py:37
  68.2 84.4 %all-gather.2.cloned.1.call-done = bf16[2,2048,768]{2,1,0:T(8,128)(2,1)} async-done(((bf16[2,512,768]{2,1,0:T(8,128)(2,1)}), bf16[2,2048,768]{2,1,0:T(8,128)(2,1)}) %all-gather.2.cloned.1.call-update) | async-done | bytes 6291472 | tf_op jit(solution)/shard_map/all_gather | solution.py:36
  152.7 11.9 %select_convert_fusion = bf16[2,2048,1024]{2,1,0:T(8,128)(2,1)S(1)} fusion(s32[1024]{0:T(1024)S(1)} %iota_add_fusion, s32[2,2048]{1,0:T(2,128)S(1)} %all_gather.6, pred[2,2048]{1,0:T(4,128)(4,1)S(1)} %broadcast_compare_fusion, bf16[2,2048,768]{2,1,0:T(8,128)(2,1)} %all-gather.2.cloned.1.call-done, bf16[2,1024,768]{2,1,0:T(8,128)(2,1)} %param.8), kind=kOutput, calls=%fused_computation.3 | convolution fusion | flops 6476005376 | bytes 17850368 | tf_op jit(solution)/shard_map/crd,cbd->crb/dot_general | solution.py:40
  164.5 3.2 copy-done.3
  167.8 8.6 %convolution_convert_fusion = bf16[2,2048,768]{2,1,0:T(8,128)(2,1)} fusion(bf16[2,2048,1024]{2,1,0:T(8,128)(2,1)S(1)} %select_convert_fusion, bf16[2,1024,768]{2,1,0:T(8,128)(2,1)S(1)} %copy-done.2), kind=kOutput, calls=%fused_computation.6 | convolution fusion | flops 6445596672 | bytes 17825792 | tf_op jit(solution)/shard_map/crb,cbd->crd/dot_general | solution.py:44
  176.4 111.4 %reduce-scatter.2.cloned.1.call-done = bf16[2,512,768]{2,1,0:T(8,128)(2,1)} async-done(((bf16[2,2048,768]{2,1,0:T(8,128)(2,1)}), bf16[2,512,768]{2,1,0:T(8,128)(2,1)}) %reduce-scatter.2.cloned.1.call-update) | async-done | bytes 1572880 | tf_op jit(solution)/shard_map/reduce_scatter | solution.py:46
  287.8 4.2 %copy.34 = bf16[2,512,768]{2,0,1:T(2,128)(2,1)} copy(bf16[2,512,768]{2,1,0:T(8,128)(2,1)} %reduce-scatter.2.cloned.1.call-done) | data formatting | bytes 3145728 | tf_op jit(solution)/shard_map/reduce_scatter | solution.py:46
  292.0 4.4 %all-to-all-start.2 = ((bf16[2,512,768]{2,0,1:T(2,128)(2,1)}), bf16[2,512,768]{2,0,1:T(2,128)(2,1)S(1)}, u32[]{:S(2)}, u32[]{:S(2)}) async-start(bf16[2,512,768]{2,0,1:T(2,128)(2,1)} %copy.34), calls=%async_computation.3 | async-start | bytes 3145728 | tf_op jit(solution)/shard_map/all_to_all | solution.py:49
  296.4 15.4 %subtract_convert_fusion = (bf16[2,1024,768]{2,1,0:T(8,128)(2,1)}, f32[2,1024,768]{2,1,0:T(8,128)}) fusion(bf16[2,1024,768]{2,1,0:T(8,128)(2,1)} %param.8, bf16[2,2048,1024]{2,1,0:T(8,128)(2,1)} %copy-done.3, bf16[2,2048,768]{2,1,0:T(8,128)(2,1)} %all-gather.2.cloned.1.call-done, f32[2,1024,768]{2,1,0:T(8,128)} %param.9), kind=kOutput, calls=%fused_computation.4 | convolution fusion | flops 6451888128 | bytes 33554432 | tf_op jit(solution)/shard_map/crb,crd->cbd/dot_general | solution.py:45
  311.8 2.2 all-to-all-done.2
  314.0 1.2 copy-done
  315.1 1.8 copy.35
  316.9 2.6 gather_fusion
  319.5 1.8 reshape.85
  321.3 1.8 reduce_sum.22
  (26 shorter events, 0.9 us)
Async XLA Ops:
  7.2 33.0 %copy-start.1 = (s32[128,4]{0,1:T(4,128)S(1)}, s32[128,4]{0,1:T(4,128)}, u32[]{:S(2)}) copy-start(s32[128,4]{0,1:T(4,128)} %param.7) | copy-start | bytes 6148
  7.2 145.5 %all-gather.2.cloned.1.call-start = ((), (), s32[]{:S(2)}) async-start(), calls=%async_computation.4 | async-start | bytes 7864320 | tf_op jit(solution)/shard_map/all_gather | solution.py:36
  43.6 8.8 %all-to-all-start = ((s32[8,1,128]{2,1,0:T(1,128)}), s32[8,1,128]{2,1,0:T(1,128)S(1)}, u32[]{:S(2)}, u32[]{:S(2)}) async-start(s32[8,1,128]{2,1,0:T(1,128)} %reshape.117), calls=%async_computation | async-start | bytes 8192 | tf_op jit(solution)/shard_map/all_to_all | solution.py:33
  48.1 239.8 %reduce-scatter.2.cloned.1.call-start = ((), (), s32[]{:S(2)}) async-start(), calls=%async_computation.5 | async-start | bytes 7864320 | tf_op jit(solution)/shard_map/reduce_scatter | solution.py:46
  68.2 99.6 %copy-start.2 = (bf16[2,1024,768]{2,1,0:T(8,128)(2,1)S(1)}, bf16[2,1024,768]{2,1,0:T(8,128)(2,1)}, u32[]{:S(2)}) copy-start(bf16[2,1024,768]{2,1,0:T(8,128)(2,1)} %param.8) | copy-start | bytes 9437188
  164.5 3.2 copy-start.3
  292.0 22.0 %all-to-all-start.2 = ((bf16[2,512,768]{2,0,1:T(2,128)(2,1)}), bf16[2,512,768]{2,0,1:T(2,128)(2,1)S(1)}, u32[]{:S(2)}, u32[]{:S(2)}) async-start(bf16[2,512,768]{2,0,1:T(2,128)(2,1)} %copy.34), calls=%async_computation.3 | async-start | bytes 3145728 | tf_op jit(solution)/shard_map/all_to_all | solution.py:49
  314.0 1.2 copy-start
Sparse Core Ops, SparseCore 0:
  40.3 112.3 all-gather.1
  176.5 111.2 reduce-scatter.1
where the time goes:
time: 335 us; the launch traced here: 330 us
  waiting for transfers between devices  202 us (60%)
  blocking collectives  38.3 us (11%)
  matrix products  35.8 us (11%)
  local copies, waits for them, and re-layouts  25.8 us (8%)
  between operations  14.2 us (4%)
  starting transfers between devices  8.86 us (3%)
  other arithmetic  4.43 us (1%)
    reduce_scatter x1, waiting for transfers between devices, shards(): lax.psum_scatter(partial_grad.astype(jnp.bfloat16), 'lab', scatter_dimens...  111 us
    all_gather x1, waiting for transfers between devices, shards(): lax.all_gather(landed, 'lab', axis=1, tiled=True)  84.4 us
    all_to_all x1, blocking collectives, shards(): lax.all_to_all(outbox, 'clus', split_axis=0, concat_axis=1, tiled=True)  23.9 us
    dot_general x1, matrix products, shards(): jnp.einsum('crb,crd->cbd', grad, arrived, preferred_element_type=jnp.floa...  15.4 us
    all_gather x1, blocking collectives, shards(): lax.all_gather(landed_tags, 'lab', axis=1, tiled=True)  14.4 us
    dot_general x1, matrix products, shards(): jnp.einsum('crd,cbd->crb', arrived, weights, preferred_element_type=jnp.f...  11.9 us
    dot_general x1, matrix products, shards(): jnp.einsum('crb,cbd->crd', grad, weights, preferred_element_type=jnp.floa...  8.58 us
  transfers between devices with their start and end apart: 4, of which 4 were waited for; matrix products, arithmetic and copies ran while one was open for 6% of the time, Pallas kernels for 0%

commit v1 on v0

--- a/solution.py
+++ b/solution.py
@@ -1,10 +1,339 @@
+import functools
+
 import jax
 import jax.numpy as jnp
 from jax import lax
+from jax.experimental import pallas as pl
+from jax.experimental.pallas import tpu as pltpu
 from jax.sharding import PartitionSpec as P
 
 momentum_decay = 0.9
 step_rate = 0.002
+BASE = 256
+TAG_ROWS = 16
+MESH = pl.DeviceIdType.MESH
+
+
+def kernel(
+    dims, blk_ref, w_hbm, m_hbm, out_ref, wn_hbm, mn_hbm,
+    Q, A, G, R, RC, RD, RX, RY, RZ, W, M, PT, PS, TG, ssem, rsem, lsem, osem,
+):
+    n_lab, cap = dims
+    planes = Q.shape[1]
+    nz = Q.shape[2]
+    q_count, width = R.shape[3:]
+    clus_local, labels, _ = W.shape
+    slots = clus_local * cap
+    blocks = 2 * nz
+    rows = blocks * cap
+    f32, bf16 = jnp.float32, jnp.bfloat16
+
+    clus, lab = lax.axis_index("clus"), lax.axis_index("lab")
+    core = clus % 2
+    sib = (clus + 1 - 2 * core, lab)
+    xn = (clus + 2 - 4 * ((clus // 2) % 2), lab)
+    yn = (clus + 4 - 8 * ((clus // 4) % 2), lab)
+    zn = lambda d: (clus, (lab + d) % n_lab)
+
+    def rc(src, dst, i, dev):
+        return pltpu.make_async_remote_copy(
+            src_ref=src, dst_ref=dst, send_sem=ssem.at[i], recv_sem=rsem.at[i],
+            device_id=dev, device_id_type=MESH,
+        )
+
+    o = 0
+    ag_z = {d: rc(Q.at[0, 0, 0], Q.at[0, 0, d], o + d - 1, zn(nz - d)) for d in range(1, nz)}
+    o += nz - 1
+    ag_x = [rc(Q.at[0, 0, d], Q.at[0, 1, d], o + d, xn) for d in range(nz)]
+    o += nz
+    ag_y = [rc(Q.at[0, 0, d], Q.at[0, 2, d], o + d, yn) for d in range(nz)]
+    o += nz
+    via_x = [d < nz // 2 for d in range(nz)]
+    ag_d = [
+        rc(Q.at[0, 1, d], Q.at[0, 3, d], o + d, yn)
+        if via_x[d]
+        else rc(Q.at[0, 2, d], Q.at[0, 3, d], o + d, xn)
+        for d in range(nz)
+    ]
+    o += nz
+    ag_s = [rc(Q.at[0, p], Q.at[1, p], o + p, sib) for p in range(planes)]
+    o += planes
+    rs_c = [rc(R.at[1, p], RC.at[p], o + p, sib) for p in range(planes)]
+    o += planes
+    rs_d = [rc(R.at[0, 3, d], RD.at[d], o + d, xn if via_x[d] else yn) for d in range(nz)]
+    o += nz
+    rs_x = [rc(R.at[0, 1, d], RX.at[d], o + d, xn) for d in range(nz)]
+    o += nz
+    rs_y = [rc(R.at[0, 2, d], RY.at[d], o + d, yn) for d in range(nz)]
+    o += nz
+    rs_z = {d: rc(R.at[0, 0, d], RZ.at[d - 1], o + d - 1, zn(d)) for d in range(1, nz)}
+
+    own = pltpu.make_async_copy(blk_ref, Q.at[0, 0, 0], lsem.at[0])
+    w_in = pltpu.make_async_copy(w_hbm, W, lsem.at[1])
+    m_in = pltpu.make_async_copy(m_hbm, M, lsem.at[2])
+    own.start()
+    w_in.start()
+    m_in.start()
+
+    barrier = pltpu.get_barrier_semaphore()
+    greet = [sib, xn, yn] + [zn(d) for d in range(1, nz)]
+    for dev in greet:
+        pl.semaphore_signal(barrier, inc=1, device_id=dev, device_id_type=MESH)
+    pl.semaphore_wait(barrier, len(greet))
+
+    own.wait()
+    for d in range(1, nz):
+        ag_z[d].start()
+    ag_x[0].start()
+    ag_y[0].start()
+    for d in sorted(range(1, nz), key=lambda d: min(d, nz - d)):
+        ag_z[d].wait_recv()
+        ag_x[d].start()
+        ag_y[d].start()
+    ag_s[0].start()
+    w_in.wait()
+
+    iota_s = lax.broadcasted_iota(jnp.int32, (slots, q_count), 0).astype(f32)
+    first = lax.broadcasted_iota(jnp.int32, (TAG_ROWS, q_count), 0)
+    earlier = (
+        lax.broadcasted_iota(jnp.int32, (q_count, q_count), 0)
+        < lax.broadcasted_iota(jnp.int32, (q_count, q_count), 1)
+    ).astype(f32).astype(bf16)
+    base = (clus * clus_local).astype(f32)
+    tile = 256
+
+    def chunk(p):
+        for b in range(blocks):
+            c, d = b // nz, b % nz
+            tags = Q[c, p, d, q_count:q_count + TAG_ROWS, 0:q_count].astype(f32)
+            here, spot = [], []
+            member = jnp.zeros((TAG_ROWS, q_count), f32)
+            for j in range(clus_local):
+                m = jnp.zeros((1, q_count), f32)
+                pos = jnp.zeros((1, q_count), f32)
+                for k in range(4):
+                    hit = tags[k:k + 1] == base + j
+                    m += jnp.where(hit, 1.0, 0.0)
+                    pos += jnp.where(hit, tags[4 + k:5 + k] * BASE + tags[8 + k:9 + k] + 1.0, 0.0)
+                here.append(m)
+                spot.append(pos)
+                member = jnp.where(first == j, jnp.broadcast_to(m, member.shape), member)
+            rank = jnp.dot(member.astype(bf16), earlier, preferred_element_type=f32)
+            pick = jnp.zeros((slots, q_count), f32)
+            mark = jnp.zeros((slots, q_count), f32)
+            for j in range(clus_local):
+                goal = jnp.where(here[j] > 0.0, rank[j:j + 1] + float(j * cap), -1.0)
+                same = iota_s == goal
+                pick = jnp.where(same, 1.0, pick)
+                mark = jnp.where(same, jnp.broadcast_to(spot[j], mark.shape), mark)
+            pick = pick.astype(bf16)
+            PT[b] = pick
+            tag = jnp.sum(mark, axis=1, keepdims=True) - 1.0
+            rowsq = jnp.dot(pick, Q[c, p, d, 0:q_count, :], preferred_element_type=f32).astype(bf16)
+            for j in range(clus_local):
+                A[j, p, b * cap:(b + 1) * cap, :] = rowsq[j * cap:(j + 1) * cap]
+                TG[j, b * cap:(b + 1) * cap, :] = jnp.broadcast_to(
+                    tag[j * cap:(j + 1) * cap], (cap, 128)
+                )
+        place = (lab * labels).astype(f32)
+
+        @pl.loop(0, clus_local)
+        def _(j):
+            a = A[j, p]
+            tag = TG[j][:, 0:1] - place
+            for n in range(0, labels, tile):
+                logits = lax.dot_general(
+                    a, W[j, n:n + tile, :], (((1,), (1,)), ((), ())), preferred_element_type=f32
+                )
+                ids = lax.broadcasted_iota(jnp.int32, (rows, tile), 1).astype(f32) + float(n)
+                g = 0.5 * jnp.tanh(0.5 * logits) + 0.5
+                G[j, p, :, n:n + tile] = jnp.where(tag == ids, g - 1.0, g).astype(bf16)
+            part = jnp.dot(G[j, p], W[j], preferred_element_type=f32).astype(bf16)
+            PS[:, pl.ds(pl.multiple_of(j * cap, cap), cap), :] = part.reshape(blocks, cap, width)
+
+        for b in range(blocks):
+            R[b // nz, p, b % nz] = lax.dot_general(
+                PT[b], PS[b], (((0,), (0,)), ((), ())), preferred_element_type=f32
+            ).astype(bf16)
+
+    def add_into(p, d, *others):
+        s = R[0, p, d].astype(f32)
+        for ref in others:
+            s = s + ref.astype(f32)
+        R[0, p, d] = s.astype(bf16)
+
+    @pl.loop(0, planes)
+    def _(p):
+        @pl.when(p == 0)
+        def _():
+            ag_s[0].wait_recv()
+
+        @pl.when(p == 1)
+        def _():
+            for d in range(nz):
+                if via_x[d]:
+                    ag_x[d].wait_recv()
+                else:
+                    ag_y[d].wait_recv()
+                ag_d[d].start()
+            for d in range(nz):
+                if not via_x[d]:
+                    ag_x[d].wait_recv()
+            ag_s[1].start()
+            for d in range(nz):
+                if via_x[d]:
+                    ag_y[d].wait_recv()
+            ag_s[2].start()
+            ag_s[1].wait_recv()
+
+        @pl.when(p == 2)
+        def _():
+            for d in range(nz):
+                ag_d[d].wait_recv()
+            ag_s[3].start()
+            ag_s[2].wait_recv()
+
+        @pl.when(p == 3)
+        def _():
+            rs_c[1].wait_recv()
+            for d in range(nz):
+                add_into(1, d, RC[1, d])
+                if via_x[d]:
+                    rs_x[d].start()
+            ag_s[3].wait_recv()
+
+        chunk(p)
+        for i in range(planes):
+            @pl.when(p == i)
+            def _(i=i):
+                rs_c[i].start()
+
+    rs_c[2].wait_recv()
+    for d in range(nz):
+        add_into(2, d, RC[2, d])
+        if not via_x[d]:
+            rs_y[d].start()
+    rs_c[3].wait_recv()
+    for d in range(nz):
+        add_into(3, d, RC[3, d])
+        rs_d[d].start()
+    rs_c[0].wait_recv()
+    for d in range(nz):
+        add_into(0, d, RC[0, d])
+    m_in.wait()
+
+    lt = 256
+    per = labels // lt
+    steps = clus_local * per
+
+    def outs(i):
+        j, n = i // per, pl.multiple_of((i % per) * lt, lt)
+        where = (j, pl.ds(n, lt))
+        return (
+            pltpu.make_async_copy(M.at[where], mn_hbm.at[where], osem.at[0, i]),
+            pltpu.make_async_copy(W.at[where], wn_hbm.at[where], osem.at[1, i]),
+        )
+
+    def update(lo, hi):
+        @pl.loop(lo, hi)
+        def _(i):
+            j, n = i // per, pl.multiple_of((i % per) * lt, lt)
+            g = G[j, :, :, pl.ds(n, lt)].reshape(planes * rows, lt)
+            a = A[j].reshape(planes * rows, width)
+            lg = lax.dot_general(g, a, (((0,), (0,)), ((), ())), preferred_element_type=f32)
+            mn = momentum_decay * M[j, pl.ds(n, lt), :] + lg
+            wn = W[j, pl.ds(n, lt), :].astype(f32) - step_rate * mn
+            M[j, pl.ds(n, lt), :] = mn
+            W[j, pl.ds(n, lt), :] = wn.astype(bf16)
+            for cp in outs(i):
+                cp.start()
+
+    update(0, steps // 4)
+    for d in range(nz):
+        rs_d[d].wait_recv()
+        if via_x[d]:
+            add_into(2, d, RD[d])
+            rs_y[d].start()
+        else:
+            add_into(1, d, RD[d])
+            rs_x[d].start()
+    update(steps // 4, steps * 3 // 4)
+    for d in list(range(1, nz)) + [0]:
+        rs_x[d].wait_recv()
+        rs_y[d].wait_recv()
+        if d:
+            add_into(0, d, RX[d], RY[d])
+            rs_z[d].start()
+    update(steps * 3 // 4, steps)
+    total = R[0, 0, 0].astype(f32) + RX[0].astype(f32) + RY[0].astype(f32)
+    for d in range(1, nz):
+        rs_z[d].wait_recv()
+        total = total + RZ[d - 1].astype(f32)
+    out_ref[...] = total
+
+    for cp in (
+        list(ag_z.values()) + ag_x + ag_y + ag_d + ag_s
+        + rs_c + rs_d + rs_x + rs_y + list(rs_z.values())
+    ):
+        cp.wait_send()
+
+    @pl.loop(0, steps)
+    def _(i):
+        for cp in outs(i):
+            cp.wait()
+
+
+def fused(queries, visits, positives, weights, momentum):
+    n_clus, n_lab = lax.axis_size("clus"), lax.axis_size("lab")
+    q_count, width = queries.shape
+    visit_count = visits.shape[1]
+    clus_local, labels, _ = weights.shape
+    cap = 2 * q_count * visit_count // (clus_local * n_clus)
+    planes = n_clus // 2
+    slots = clus_local * cap
+    bf16, f32 = jnp.bfloat16, jnp.float32
+    vt, pt = visits.T, positives.T
+    tags = jnp.concatenate([vt, pt // BASE, pt % BASE], axis=0).astype(bf16)
+    tags = jnp.pad(tags, ((0, TAG_ROWS - tags.shape[0]), (0, width - q_count)))
+    blk = jnp.concatenate([queries, tags], axis=0)
+    rows = 2 * n_lab * cap
+    n_sem = 2 * (2 * (n_lab - 1) // 2) + 6 * n_lab + 2 * planes
+    blocks = lambda *lead: pltpu.VMEM(lead + (q_count, width), bf16)
+    any_spec = pl.BlockSpec(memory_space=pl.ANY)
+    steps = clus_local * (labels // 256)
+    return pl.pallas_call(
+        functools.partial(kernel, (n_lab, cap)),
+        out_shape=(
+            jax.ShapeDtypeStruct((q_count, width), f32),
+            jax.ShapeDtypeStruct(weights.shape, bf16),
+            jax.ShapeDtypeStruct(momentum.shape, f32),
+        ),
+        in_specs=[any_spec] * 3,
+        out_specs=(pl.BlockSpec(memory_space=pltpu.VMEM), any_spec, any_spec),
+        scratch_shapes=[
+            pltpu.VMEM((2, planes, n_lab, q_count + TAG_ROWS, width), bf16),
+            pltpu.VMEM((clus_local, planes, rows, width), bf16),
+            pltpu.VMEM((clus_local, planes, rows, labels), bf16),
+            blocks(2, planes, n_lab),
+            blocks(planes, n_lab),
+            blocks(n_lab),
+            blocks(n_lab),
+            blocks(n_lab),
+            blocks(n_lab - 1),
+            pltpu.VMEM(weights.shape, bf16),
+            pltpu.VMEM(momentum.shape, f32),
+            pltpu.VMEM((2 * n_lab, slots, q_count), bf16),
+            pltpu.VMEM((2 * n_lab, slots, width), bf16),
+            pltpu.VMEM((clus_local, rows, 128), f32),
+            pltpu.SemaphoreType.DMA((n_sem,)),
+            pltpu.SemaphoreType.DMA((n_sem,)),
+            pltpu.SemaphoreType.DMA((3,)),
+            pltpu.SemaphoreType.DMA((2, steps)),
+        ],
+        compiler_params=pltpu.CompilerParams(
+            collective_id=0, has_side_effects=True, vmem_limit_bytes=63 * 1024 * 1024
+        ),
+    )(blk, weights, momentum)
 
 
 def shards(queries, visits, positives, weights, momentum):
@@ -65,4 +394,6 @@
         P("clus", "lab", None),
     )
     out_specs = (P(("clus", "lab"), None), P("clus", "lab", None), P("clus", "lab", None))
-    return jax.shard_map(shards, mesh=mesh, in_specs=in_specs, out_specs=out_specs, check_vma=False)
+    planes = mesh.shape["clus"] // 2
+    step = fused if planes == 4 else shards
+    return jax.shard_map(step, mesh=mesh, in_specs=in_specs, out_specs=out_specs, check_vma=False)

time: 335 us -> 115 us (0.34); the launches traced: 330 us -> 114 us
  waiting for transfers between devices: 202 us -> 0 us
  Pallas kernels: 0 us -> 102 us
  blocking collectives: 38.3 us -> 0 us
  matrix products: 35.8 us -> 0 us
  local copies, waits for them, and re-layouts: 25.8 us -> 8.53 us
  between operations: 14.2 us -> 0.65 us
  starting transfers between devices: 8.86 us -> 0 us
    reduce_scatter x1 -> x0, waiting for transfers between devices: 111 us -> none  [shards(): lax.psum_scatter(partial_grad.astype(jnp.bfloat16), 'lab', scatter_dimens...]
    pallas_call x0 -> x1, Pallas kernels: none -> 102 us  [fused(): pl.pallas_call(functools.partial(kernel, (n_lab, cap)), out_shape=(jax.Sh...]
    all_gather x1 -> x0, waiting for transfers between devices: 84.4 us -> none  [shards(): lax.all_gather(landed, 'lab', axis=1, tiled=True)]
    dot_general x3 -> x0, matrix products: 35.8 us -> none  [the longest x1 15.4 us: shards(): jnp.einsum('crb,crd->cbd', grad, arrived, preferred_element_type=jnp.floa...]
    all_to_all x1 -> x0, blocking collectives: 23.9 us -> none  [shards(): lax.all_to_all(outbox, 'clus', split_axis=0, concat_axis=1, tiled=True)]
    all_gather x1 -> x0, blocking collectives: 14.4 us -> none  [shards(): lax.all_gather(landed_tags, 'lab', axis=1, tiled=True)]
    all_to_all x2 -> x0, starting transfers between devices: 8.82 us -> none  [the longest x1 4.44 us: shards(): lax.all_to_all(out_tags, 'clus', split_axis=0, concat_axis=1, tiled=True)]
    all_to_all x2 -> x0, waiting for transfers between devices: 6.54 us -> none  [the longest x1 4.34 us: shards(): lax.all_to_all(out_tags, 'clus', split_axis=0, concat_axis=1, tiled=True)]
  transfers between devices with their start and end apart: 4 -> 0, of which waited for: 4 -> 0; matrix products, arithmetic and copies ran while one was open for 6% -> 0% of each run, Pallas kernels for 0% -> 0%
where the time goes in v1:
time: 115 us; the launch traced here: 114 us
  Pallas kernels  102 us (89%)
  local copies, waits for them, and re-layouts  8.53 us (7%)
  other arithmetic  3.02 us (3%)
    pallas_call x1, Pallas kernels, fused(): pl.pallas_call(functools.partial(kernel, (n_lab, cap)), out_shape=(jax.Sh...  102 us
    unnamed x5, local copies, waits for them, and re-layouts  8.53 us

profile of v1, /device:TPU:25, one launch (start us, length us, event | category | flops | bytes accessed | tf_op | source)
XLA Modules:
  0.0 114.5 jit_solution(3975910690416945415)
XLA Ops:
  0.6 0.7 convert_bitcast_fusion
  1.3 0.7 fusion.9
  2.0 1.6 %pad_maximum_fusion.blk_ref = bf16[144,768]{1,0:T(8,128)(2,1)} fusion(bf16[16,768]{1,0:T(8,128)(2,1)S(1)} %fusion.8, bf16[128,768]{1,0:T(8,128)(2,1)} %param.5), kind=kLoop, calls=%fused_computation | loop fusion | flops 442368 | bytes 442368 | tf_op jit(solution)/shard_map/concatenate | solution.py:298
  3.6 102.3 %shard_map.76 = (f32[128,768]{1,0:T(8,128)}, bf16[2,1024,768]{2,1,0:T(8,128)(2,1)}, f32[2,1024,768]{2,1,0:T(8,128)}) custom-call(bf16[144,768]{1,0:T(8,128)(2,1)} %pad_maximum_fusion.blk_ref, bf16[2,1024,768]{2,1,0:T(8,128)(2,1)} %w_hbm.1, f32[2,1024,768]{2,1,0:T(8,128)} %m_hbm.1), custom_call_target="tpu_custom_call" | custom-call | tf_op jit(solution)/shard_map/pallas_call | solution.py:304
  105.9 0.0 copy-start
  105.9 1.9 %copy.11 = f32[128,768]{1,0:T(8,128)} copy(f32[128,768]{1,0:T(8,128)} %get-tuple-element.8) | data formatting | bytes 786432
  107.9 3.9 %copy.12 = bf16[2,1024,768]{2,1,0:T(8,128)(2,1)} copy(bf16[2,1024,768]{2,1,0:T(8,128)(2,1)} %get-tuple-element.9) | data formatting | bytes 6291456
  111.8 0.0 copy-done
  111.8 2.7 %copy.13 = f32[2,1024,768]{2,1,0:T(8,128)} copy(f32[2,1024,768]{2,1,0:T(8,128)S(1)} %copy-done) | data formatting | bytes 12582912
  (1 shorter events, 0.0 us)
Async XLA Ops:
  105.9 5.8 %copy-start = (f32[2,1024,768]{2,1,0:T(8,128)S(1)}, f32[2,1024,768]{2,1,0:T(8,128)}, u32[]{:S(2)}) copy-start(f32[2,1024,768]{2,1,0:T(8,128)} %get-tuple-element.10) | copy-start | bytes 18874372

commit v2 on v1

--- a/solution.py
+++ b/solution.py
@@ -15,7 +15,7 @@
 
 
 def kernel(
-    dims, blk_ref, w_hbm, m_hbm, out_ref, wn_hbm, mn_hbm,
+    dims, q_hbm, t_hbm, w_hbm, m_hbm, out_ref, wn_hbm, mn_hbm,
     Q, A, G, R, RC, RD, RX, RY, RZ, W, M, PT, PS, TG, ssem, rsem, lsem, osem,
 ):
     n_lab, cap = dims
@@ -56,10 +56,15 @@
         for d in range(nz)
     ]
     o += nz
-    ag_s = [rc(Q.at[0, p], Q.at[1, p], o + p, sib) for p in range(planes)]
-    o += planes
-    rs_c = [rc(R.at[1, p], RC.at[p], o + p, sib) for p in range(planes)]
-    o += planes
+    ag_s = [rc(Q.at[0, p], Q.at[1, p], o + p, sib) for p in range(planes - 1)]
+    o += planes - 1
+    ag_f = [rc(Q.at[0, 3, d], Q.at[1, 3, d], o + d, sib) for d in range(nz)]
+    o += nz
+    rs_c = [rc(R.at[1, p], RC.at[p], o + p, sib) for p in range(planes - 1)]
+    o += planes - 1
+    rs_f = [rc(R.at[1, 3, d], RC.at[3, d], o + d, sib) for d in range(nz)]
+    o += nz
+    late = [d for d in (1, 2, 0) if d < nz] + list(range(3, nz))
     rs_d = [rc(R.at[0, 3, d], RD.at[d], o + d, xn if via_x[d] else yn) for d in range(nz)]
     o += nz
     rs_x = [rc(R.at[0, 1, d], RX.at[d], o + d, xn) for d in range(nz)]
@@ -68,10 +73,12 @@
     o += nz
     rs_z = {d: rc(R.at[0, 0, d], RZ.at[d - 1], o + d - 1, zn(d)) for d in range(1, nz)}
 
-    own = pltpu.make_async_copy(blk_ref, Q.at[0, 0, 0], lsem.at[0])
+    own = pltpu.make_async_copy(q_hbm, Q.at[0, 0, 0, pl.ds(0, q_count)], lsem.at[0])
+    own_tags = pltpu.make_async_copy(t_hbm, Q.at[0, 0, 0, pl.ds(q_count, TAG_ROWS)], lsem.at[3])
     w_in = pltpu.make_async_copy(w_hbm, W, lsem.at[1])
     m_in = pltpu.make_async_copy(m_hbm, M, lsem.at[2])
     own.start()
+    own_tags.start()
     w_in.start()
     m_in.start()
 
@@ -82,15 +89,27 @@
     pl.semaphore_wait(barrier, len(greet))
 
     own.wait()
-    for d in range(1, nz):
-        ag_z[d].start()
+    own_tags.wait()
+    near = sorted(range(1, nz), key=lambda d: min(d, nz - d))
     ag_x[0].start()
     ag_y[0].start()
-    for d in sorted(range(1, nz), key=lambda d: min(d, nz - d)):
+    for d in near:
+        ag_z[d].start()
+
+    def turn(d):
+        (ag_x if via_x[d] else ag_y)[d].wait_recv()
+        ag_d[d].start()
+
+    ag_z[near[0]].wait_recv()
+    ag_x[near[0]].start()
+    ag_y[near[0]].start()
+    turn(0)
+    for d in near[1:]:
         ag_z[d].wait_recv()
         ag_x[d].start()
         ag_y[d].start()
     ag_s[0].start()
+    turn(near[0])
     w_in.wait()
 
     iota_s = lax.broadcasted_iota(jnp.int32, (slots, q_count), 0).astype(f32)
@@ -170,12 +189,8 @@
 
         @pl.when(p == 1)
         def _():
-            for d in range(nz):
-                if via_x[d]:
-                    ag_x[d].wait_recv()
-                else:
-                    ag_y[d].wait_recv()
-                ag_d[d].start()
+            for d in near[1:]:
+                turn(d)
             for d in range(nz):
                 if not via_x[d]:
                     ag_x[d].wait_recv()
@@ -190,7 +205,7 @@
         def _():
             for d in range(nz):
                 ag_d[d].wait_recv()
-            ag_s[3].start()
+                ag_f[d].start()
             ag_s[2].wait_recv()
 
         @pl.when(p == 3)
@@ -200,21 +215,26 @@
                 add_into(1, d, RC[1, d])
                 if via_x[d]:
                     rs_x[d].start()
-            ag_s[3].wait_recv()
+            for d in range(nz):
+                ag_f[d].wait_recv()
 
         chunk(p)
         for i in range(planes):
             @pl.when(p == i)
             def _(i=i):
-                rs_c[i].start()
+                if i < 3:
+                    rs_c[i].start()
+                else:
+                    for d in late:
+                        rs_f[d].start()
 
     rs_c[2].wait_recv()
     for d in range(nz):
         add_into(2, d, RC[2, d])
         if not via_x[d]:
             rs_y[d].start()
-    rs_c[3].wait_recv()
-    for d in range(nz):
+    for d in late:
+        rs_f[d].wait_recv()
         add_into(3, d, RC[3, d])
         rs_d[d].start()
     rs_c[0].wait_recv()
@@ -249,7 +269,7 @@
                 cp.start()
 
     update(0, steps // 4)
-    for d in range(nz):
+    for d in late:
         rs_d[d].wait_recv()
         if via_x[d]:
             add_into(2, d, RD[d])
@@ -257,14 +277,14 @@
         else:
             add_into(1, d, RD[d])
             rs_x[d].start()
-    update(steps // 4, steps * 3 // 4)
-    for d in list(range(1, nz)) + [0]:
+    update(steps // 4, steps * 5 // 8)
+    for d in [d for d in late if d] + [0]:
         rs_x[d].wait_recv()
         rs_y[d].wait_recv()
         if d:
             add_into(0, d, RX[d], RY[d])
             rs_z[d].start()
-    update(steps * 3 // 4, steps)
+    update(steps * 5 // 8, steps)
     total = R[0, 0, 0].astype(f32) + RX[0].astype(f32) + RY[0].astype(f32)
     for d in range(1, nz):
         rs_z[d].wait_recv()
@@ -272,8 +292,8 @@
     out_ref[...] = total
 
     for cp in (
-        list(ag_z.values()) + ag_x + ag_y + ag_d + ag_s
-        + rs_c + rs_d + rs_x + rs_y + list(rs_z.values())
+        list(ag_z.values()) + ag_x + ag_y + ag_d + ag_s + ag_f
+        + rs_c + rs_f + rs_d + rs_x + rs_y + list(rs_z.values())
     ):
         cp.wait_send()
 
@@ -295,9 +315,8 @@
     vt, pt = visits.T, positives.T
     tags = jnp.concatenate([vt, pt // BASE, pt % BASE], axis=0).astype(bf16)
     tags = jnp.pad(tags, ((0, TAG_ROWS - tags.shape[0]), (0, width - q_count)))
-    blk = jnp.concatenate([queries, tags], axis=0)
     rows = 2 * n_lab * cap
-    n_sem = 2 * (2 * (n_lab - 1) // 2) + 6 * n_lab + 2 * planes
+    n_sem = 2 * (2 * (n_lab - 1) // 2) + 8 * n_lab + 2 * (planes - 1)
     blocks = lambda *lead: pltpu.VMEM(lead + (q_count, width), bf16)
     any_spec = pl.BlockSpec(memory_space=pl.ANY)
     steps = clus_local * (labels // 256)
@@ -308,7 +327,7 @@
             jax.ShapeDtypeStruct(weights.shape, bf16),
             jax.ShapeDtypeStruct(momentum.shape, f32),
         ),
-        in_specs=[any_spec] * 3,
+        in_specs=[any_spec] * 4,
         out_specs=(pl.BlockSpec(memory_space=pltpu.VMEM), any_spec, any_spec),
         scratch_shapes=[
             pltpu.VMEM((2, planes, n_lab, q_count + TAG_ROWS, width), bf16),
@@ -327,13 +346,13 @@
             pltpu.VMEM((clus_local, rows, 128), f32),
             pltpu.SemaphoreType.DMA((n_sem,)),
             pltpu.SemaphoreType.DMA((n_sem,)),
-            pltpu.SemaphoreType.DMA((3,)),
+            pltpu.SemaphoreType.DMA((4,)),
             pltpu.SemaphoreType.DMA((2, steps)),
         ],
         compiler_params=pltpu.CompilerParams(
             collective_id=0, has_side_effects=True, vmem_limit_bytes=63 * 1024 * 1024
         ),
-    )(blk, weights, momentum)
+    )(queries, tags, weights, momentum)
 
 
 def shards(queries, visits, positives, weights, momentum):

time: 115 us -> 108 us (0.939)
  Pallas kernels: 102 us -> 95.4 us
    pallas_call x1, Pallas kernels: 102 us -> 95.4 us  [fused(): pl.pallas_call(functools.partial(kernel, (n_lab, cap)), out_shape=(jax.Sh...]
    concatenate x1 -> x0, other arithmetic: 1.63 us -> none  [fused(): blk = jnp.concatenate([queries, tags], axis=0)]
where the time goes in v2:
time: 108 us; the launch traced here: 107 us
  Pallas kernels  95.4 us (88%)
  local copies, waits for them, and re-layouts  8.53 us (8%)
  other arithmetic  2 us (2%)
    pallas_call x1, Pallas kernels, fused(): pl.pallas_call(functools.partial(kernel, (n_lab, cap)), out_shape=(jax.Sh...  95.4 us
    unnamed x5, local copies, waits for them, and re-layouts  8.53 us

profile of v2, /device:TPU:25, one launch (start us, length us, event | category | flops | bytes accessed | tf_op | source)
XLA Modules:
  0.0 106.6 jit_solution(3350465578526166474)
XLA Ops:
  0.6 0.7 convert_bitcast_fusion
  1.3 0.7 fusion.9
  2.0 0.6 fusion.8.t_hbm
  2.6 95.4 %shard_map.76 = (f32[128,768]{1,0:T(8,128)}, bf16[2,1024,768]{2,1,0:T(8,128)(2,1)}, f32[2,1024,768]{2,1,0:T(8,128)}) custom-call(bf16[128,768]{1,0:T(8,128)(2,1)} %q_hbm.1, bf16[16,768]{1,0:T(8,128)(2,1)} %fusion.8.t_hbm, bf16[2,1024,768]{2,1,0:T(8,128)(2,1)} %w_hbm.1, f32[2,1024,768]{2,1,0:T(8,128)} %m_hbm.1), custom_call_target="tpu_custom_call" | custom-call | tf_op jit(solution)/shard_map/pallas_call | solution.py:323
  98.0 0.0 copy-start
  98.0 1.9 %copy.11 = f32[128,768]{1,0:T(8,128)} copy(f32[128,768]{1,0:T(8,128)} %get-tuple-element.8) | data formatting | bytes 786432
  100.0 3.9 %copy.12 = bf16[2,1024,768]{2,1,0:T(8,128)(2,1)} copy(bf16[2,1024,768]{2,1,0:T(8,128)(2,1)} %get-tuple-element.9) | data formatting | bytes 6291456
  103.9 0.0 copy-done
  103.9 2.7 %copy.13 = f32[2,1024,768]{2,1,0:T(8,128)} copy(f32[2,1024,768]{2,1,0:T(8,128)S(1)} %copy-done) | data formatting | bytes 12582912
Async XLA Ops:
  98.0 5.8 %copy-start = (f32[2,1024,768]{2,1,0:T(8,128)S(1)}, f32[2,1024,768]{2,1,0:T(8,128)}, u32[]{:S(2)}) copy-start(f32[2,1024,768]{2,1,0:T(8,128)} %get-tuple-element.10) | copy-start | bytes 18874372

commit v3 on v2

--- a/solution.py
+++ b/solution.py
@@ -215,6 +215,14 @@
                 add_into(1, d, RC[1, d])
                 if via_x[d]:
                     rs_x[d].start()
+            rs_c[0].wait_recv()
+            for d in range(nz):
+                add_into(0, d, RC[0, d])
+            rs_c[2].wait_recv()
+            for d in range(nz):
+                add_into(2, d, RC[2, d])
+                if not via_x[d]:
+                    rs_y[d].start()
             for d in range(nz):
                 ag_f[d].wait_recv()
 
@@ -228,18 +236,10 @@
                     for d in late:
                         rs_f[d].start()
 
-    rs_c[2].wait_recv()
-    for d in range(nz):
-        add_into(2, d, RC[2, d])
-        if not via_x[d]:
-            rs_y[d].start()
     for d in late:
         rs_f[d].wait_recv()
         add_into(3, d, RC[3, d])
         rs_d[d].start()
-    rs_c[0].wait_recv()
-    for d in range(nz):
-        add_into(0, d, RC[0, d])
     m_in.wait()
 
     lt = 256

time: 108 us -> 104 us (0.963)
  Pallas kernels: 95.4 us -> 92.2 us
    pallas_call x1, Pallas kernels: 95.4 us -> 92.2 us  [fused(): pl.pallas_call(functools.partial(kernel, (n_lab, cap)), out_shape=(jax.Sh...]
where the time goes in v3:
time: 104 us; the launch traced here: 103 us
  Pallas kernels  92.2 us (89%)
  local copies, waits for them, and re-layouts  8.53 us (8%)
  other arithmetic  2 us (2%)
    pallas_call x1, Pallas kernels, fused(): pl.pallas_call(functools.partial(kernel, (n_lab, cap)), out_shape=(jax.Sh...  92.2 us
    unnamed x5, local copies, waits for them, and re-layouts  8.53 us

profile of v3, /device:TPU:25, one launch (start us, length us, event | category | flops | bytes accessed | tf_op | source)
XLA Modules:
  0.0 103.3 jit_solution(2787324466407295124)
XLA Ops:
  0.6 0.7 convert_bitcast_fusion
  1.3 0.7 fusion.9
  2.0 0.6 fusion.8.t_hbm
  2.6 92.2 %shard_map.76 = (f32[128,768]{1,0:T(8,128)}, bf16[2,1024,768]{2,1,0:T(8,128)(2,1)}, f32[2,1024,768]{2,1,0:T(8,128)}) custom-call(bf16[128,768]{1,0:T(8,128)(2,1)} %q_hbm.1, bf16[16,768]{1,0:T(8,128)(2,1)} %fusion.8.t_hbm, bf16[2,1024,768]{2,1,0:T(8,128)(2,1)} %w_hbm.1, f32[2,1024,768]{2,1,0:T(8,128)} %m_hbm.1), custom_call_target="tpu_custom_call" | custom-call | tf_op jit(solution)/shard_map/pallas_call | solution.py:323
  94.8 0.0 copy-start
  94.8 1.9 %copy.11 = f32[128,768]{1,0:T(8,128)} copy(f32[128,768]{1,0:T(8,128)} %get-tuple-element.8) | data formatting | bytes 786432
  96.7 3.9 %copy.12 = bf16[2,1024,768]{2,1,0:T(8,128)(2,1)} copy(bf16[2,1024,768]{2,1,0:T(8,128)(2,1)} %get-tuple-element.9) | data formatting | bytes 6291456
  100.6 0.0 copy-done
  100.6 2.7 %copy.13 = f32[2,1024,768]{2,1,0:T(8,128)} copy(f32[2,1024,768]{2,1,0:T(8,128)S(1)} %copy-done) | data formatting | bytes 12582912
Async XLA Ops:
  94.8 5.8 %copy-start = (f32[2,1024,768]{2,1,0:T(8,128)S(1)}, f32[2,1024,768]{2,1,0:T(8,128)}, u32[]{:S(2)}) copy-start(f32[2,1024,768]{2,1,0:T(8,128)} %get-tuple-element.10) | copy-start | bytes 18874372
